TPU v7x, 512 devices: a whole 4x4x16 slice. The times are simulated.
512 devices in a mesh: segment: 4 (over y_lo, core), band: 128 (over z, x, y_hi).
Axes of the slice: x: 4, y: 4 (y_hi: 2, y_lo: 2; y = y_hi * 2 + y_lo), z: 16, core: 2. Of those that a mesh axis runs over, the one named last changes fastest.
Arguments:
- voltages: bfloat16 [2, 2048, 16384], P(None, 'band', 'segment'), may hold values from -6 to 6
- slot_of_antenna: int32 [2048], replicated, may hold values from 0 to 2047, each once
- antenna_positions: int32 [2048, 2], replicated, may hold values from -1000 to 999
- beam_directions: int32 [1024, 2], replicated, may hold values from -64 to 63
Outputs:
- vis_real: float32 [128, 4, 256, 2048], P('band', 'segment')
- vis_imag: float32 [128, 4, 256, 2048], P('band', 'segment')
- beam_series: float32 [2, 4, 128, 2, 16384], P(None, 'segment', 'band')
Inputs may be any that keep to these rules, and one draw needn't show every extreme that they name: `slot_of_antenna`: a permutation of the antennas.
All inputs are finite; a program needn't handle non-finite values.
Results may differ from a plain program's by a relative error of at most 0.005.
Values may be sent and summed in bfloat16 or wider, within the bound.
A program may use at most 64 MiB of HBM per device.

v0:
```python
import math
import jax
import jax.numpy as jnp
from jax import lax
from jax.sharding import PartitionSpec as P

A = 2048
C = 64
BEAMS = 1024
NB = 256


def dft_parts():
    index = jnp.arange(64, dtype=jnp.int32)
    product = jnp.remainder(index[:, None] * index[None, :], 64).astype(jnp.float32)
    theta = product * (2.0 * math.pi / 64.0)
    return (jnp.cos(theta) * 0.125, jnp.sin(theta) * 0.125)


def forward_table():
    cosine, sine = dft_parts()
    return jnp.stack([jnp.stack([cosine, -sine], axis=1), jnp.stack([sine, cosine], axis=1)])


def inverse_table():
    cosine, sine = dft_parts()
    return jnp.stack([jnp.stack([cosine, sine], axis=1), jnp.stack([-sine, cosine], axis=1)])


def channelize(samples):
    count = samples.shape[2] // 64
    values = samples.astype(jnp.float32).reshape(2, samples.shape[1], count, 64)
    spectra = jnp.einsum(
        "pajn,pnqk->kqaj", values, forward_table(), precision=lax.Precision.HIGHEST
    )
    return spectra.astype(jnp.bfloat16)


def paired(spectra):
    doubled = jnp.broadcast_to(spectra[:, None], (spectra.shape[0], 2) + spectra.shape[1:])
    return doubled.reshape((2 * spectra.shape[0],) + spectra.shape[1:])


def steering(channel, directions, positions):
    delay = jnp.remainder(
        directions[:, 0:1] * positions[None, :, 0] + directions[:, 1:2] * positions[None, :, 1], 64
    )
    phase = jnp.remainder(channel * delay, 64).astype(jnp.float32) * (2.0 * math.pi / 64.0)
    return jnp.stack([jnp.cos(phase), -jnp.sin(phase)]).astype(jnp.bfloat16)


def resynthesize(received):
    lanes = received.shape[3]
    beams_here = received.shape[1]
    split = received.reshape(C, 2, beams_here, 2, lanes)
    series = jnp.einsum(
        "khbpj,pkqn->hbqjn", split, inverse_table(), precision=lax.Precision.HIGHEST
    )
    return series.reshape(2, beams_here, 2, lanes * 64)


def per_device(voltages, slot_of_antenna, antenna_positions, beam_directions):
    n_segment = lax.axis_size("segment")
    n_band = lax.axis_size("band")
    segment = lax.axis_index("segment")
    band = lax.axis_index("band")
    pair_count = 2 * C // n_band
    row_block = A // (2 * n_segment)
    beam_block = BEAMS // (2 * n_segment)
    beam_scale = 1.0 / math.sqrt(A)
    pair_ids = band * pair_count + jnp.arange(pair_count, dtype=jnp.int32)
    channels = pair_ids // 2
    halves = pair_ids % 2
    row_starts = (halves * n_segment + segment) * row_block
    beam_starts = halves * (n_segment * beam_block) + segment * beam_block

    def pair_weights(channel, beam_start):
        directions = lax.dynamic_slice_in_dim(beam_directions, beam_start, beam_block, 0)
        return steering(channel, directions, antenna_positions)

    weights = jax.vmap(pair_weights)(channels, beam_starts)

    def pair_terms(block, weight, row_start):
        rows = lax.dynamic_slice_in_dim(block, row_start, row_block, 1)
        turned = jnp.stack([rows[1], -rows[0]])
        left = jnp.stack([rows, turned])
        gram = jnp.einsum("gprt,pat->gra", left, block, preferred_element_type=jnp.float32)
        mixed = jnp.einsum("gba,pat->gbpt", weight, block, preferred_element_type=jnp.float32)
        formed_real = mixed[0, :, 0] - mixed[1, :, 1]
        formed_imag = mixed[0, :, 1] + mixed[1, :, 0]
        return (gram, jnp.stack([formed_real, formed_imag], axis=1) * beam_scale)

    spectra = paired(channelize(voltages))
    owned = lax.all_to_all(spectra, "band", split_axis=0, concat_axis=2, tiled=True)
    ordered = jnp.take(
        lax.all_gather(owned, "segment", axis=3, tiled=True), slot_of_antenna, axis=2
    )
    gram_part, formed_part = jax.vmap(pair_terms)(ordered, weights, row_starts)
    formed_total = formed_part
    gram_total, formed_total = (gram_part, formed_total)
    gram_total = gram_total * (1.0 / NB)
    vis_real = gram_total[:, 0][:, None]
    vis_imag = gram_total[:, 1][:, None]
    series = resynthesize(
        lax.all_to_all(
            formed_total.astype(jnp.bfloat16), "band", split_axis=1, concat_axis=0, tiled=True
        ).astype(formed_total.dtype)
    )
    beam_series = series.reshape(2, 1, series.shape[1], 2, series.shape[3])
    return (vis_real, vis_imag, beam_series)


def solution(mesh):
    in_specs = (P(None, "band", "segment"), P(), P(), P())
    out_specs = (
        P("band", "segment", None, None),
        P("band", "segment", None, None),
        P(None, "segment", "band", None, None),
    )
    return jax.shard_map(
        per_device, mesh=mesh, in_specs=in_specs, out_specs=out_specs, check_vma=False
    )
```

profile of v0, /device:TPU:32, one launch (start us, length us, event | category | flops | bytes accessed | tf_op | source)
XLA Modules:
  0.0 170.9 jit_solution(14214573905199428207)
XLA Ops:
  7.2 0.0 copy-start
  7.2 0.0 all-gather.2.cloned.1.call-start
  7.2 0.1 fusion.41
  7.4 0.2 sine_multiply_fusion
  7.5 1.5 reshape.623
  9.0 0.9 fusion.7
  9.9 0.3 copy.34
  10.3 0.2 broadcast_in_dim.34
  10.5 0.6 reshape.700
  11.1 57.2 %all_to_all.27 = bf16[128,2,1024]{2,1,0:T(2,128)(2,1)S(1)} all-to-all(bf16[128,2,1024]{2,1,0:T(2,128)(2,1)S(1)} %reshape.700), channel_id=1, replica_groups=mesh['segment'=4,'band'=128] {'band'}, dimensions={0} | all-to-all | bytes 1048576 | tf_op jit(solution)/shard_map/all_to_all | solution.py:94
  68.2 0.6 reshape.701
  68.8 0.0 copy-start.2
  68.9 0.0 copy-start.3
  68.9 0.2 copy.35
  69.1 1.3 copy.36
  70.4 0.0 all-gather.2.cloned.1.call-update
  70.4 0.0 copy-done
  70.5 5.0 %cosine_convert_fusion = (bf16[1,128,2048]{2,1,0:T(8,128)(2,1)S(1)}, bf16[1,128,2048]{2,1,0:T(8,128)(2,1)S(1)}) fusion(s32[2048]{0:T(1024)S(1)} %bitcast.117, s32[128]{0:T(128)S(1)} %get-tuple-element.51, s32[2048]{0:T(1024)S(1)} %bitcast.116, s32[128]{0:T(128)S(1)} %get-tuple-element.50, s32[]{:T(128)} %bitcast.30), kind=kLoop, calls=%fused_computation.31 | loop fusion | flops 8126464 | bytes 1065988 | tf_op jit(solution)/shard_map/convert
  75.5 20.0 %all-gather.2.cloned.1.call-done = bf16[1,2,2048,256]{2,1,0,3:T(2,128)(2,1)} async-done(((bf16[1,2,2048,64]{2,1,0,3:T(2,128)(2,1)}), bf16[1,2,2048,256]{2,1,0,3:T(2,128)(2,1)}) %all-gather.2.cloned.1.call-update) | async-done | bytes 2097168 | tf_op jit(solution)/shard_map/all_gather | solution.py:96
  95.5 8.3 %copy.37 = bf16[1,2,2048,256]{3,1,2,0:T(2,128)(2,1)S(1)} copy(bf16[1,2,2048,256]{2,1,0,3:T(2,128)(2,1)} %all-gather.2.cloned.1.call-done) | data formatting | bytes 4194304 | tf_op jit(solution)/shard_map/all_gather | solution.py:96
  103.8 16.5 %gather_fusion = bf16[2048,2,256]{2,1,0:T(2,128)(2,1)} fusion(bf16[2,2048,256]{2,0,1:T(2,128)(2,1)S(1)} %bitcast.110, s32[2048]{0:T(1024)S(1)} %fusion.42), kind=kCustom, calls=%fused_computation | custom fusion | bytes 4202496 | tf_op jit(solution)/shard_map/jit(_take)/gather | solution.py:95
  120.3 2.1 %bitcast_select_fusion = bf16[1,2,2048,256]{3,2,0,1:T(8,128)(2,1)S(1)} fusion(pred[2048]{0:T(1024)(128)(4,1)S(1)} %compare_and_fusion, bf16[2048,2,256]{2,1,0:T(2,128)(2,1)} %gather_fusion), kind=kLoop, calls=%fused_computation.3 | loop fusion | flops 1048576 | bytes 4196352 | tf_op jit(solution)/shard_map/jit(_take)/select_n | solution.py:95
  122.3 0.1 copy-done.1
  122.5 0.9 fusion.8
  123.4 0.8 copy.39
  124.2 18.6 %all-to-all-start.1 = ((bf16[1,128,2,256]{3,2,0,1:T(2,128)(2,1)}), bf16[1,128,2,256]{3,2,0,1:T(2,128)(2,1)S(1)}, u32[]{:S(2)}, u32[]{:S(2)}) async-start(bf16[1,128,2,256]{3,2,0,1:T(2,128)(2,1)} %copy.39), calls=%async_computation.1 | async-start | bytes 262144 | tf_op jit(solution)/shard_map/all_to_all | solution.py:105
  142.9 1.3 fusion
  144.2 2.3 %fusion.47 = (f32[1,1,256,2048]{3,2,1,0:T(8,128)}, f32[1,1,256,2048]{3,2,1,0:T(8,128)}) fusion(f32[1,2,256,2048]{3,2,1,0:T(8,128)S(1)} %fusion), kind=kLoop, calls=%fused_computation.84 | loop fusion | bytes 8388608 | tf_op jit(solution)/shard_map/slice | solution.py:103
  146.5 16.1 %all-to-all-done.1 = bf16[1,128,2,256]{3,2,0,1:T(2,128)(2,1)S(1)} async-done(((bf16[1,128,2,256]{3,2,0,1:T(2,128)(2,1)}), bf16[1,128,2,256]{3,2,0,1:T(2,128)(2,1)S(1)}, u32[]{:S(2)}, u32[]{:S(2)}) %all-to-all-start.1) | async-done | bytes 131104 | tf_op jit(solution)/shard_map/all_to_all | solution.py:105
  162.6 0.3 convolution_bitcast_fusion.1
  162.9 0.2 copy.42
  163.1 1.0 reshape_reshape.3
  (14 shorter events, 0.2 us)
Async XLA Ops:
  7.2 63.3 %copy-start = (s32[1024,2]{0,1:T(2,128)S(1)}, s32[1024,2]{0,1:T(2,128)}, u32[]{:S(2)}) copy-start(s32[1024,2]{0,1:T(2,128)} %param.7) | copy-start | bytes 24580
  7.2 88.3 %all-gather.2.cloned.1.call-start = ((), (), s32[]{:S(2)}) async-start(), calls=%async_computation.2 | async-start | bytes 2621440 | tf_op jit(solution)/shard_map/all_gather | solution.py:96
  68.8 1.6 copy-start.2
  68.9 1.7 copy-start.3
  120.2 2.2 %copy-start.1 = (bf16[2048,2,256]{2,1,0:T(2,128)(2,1)S(1)}, bf16[2048,2,256]{2,1,0:T(2,128)(2,1)}, u32[]{:S(2)}) copy-start(bf16[2048,2,256]{2,1,0:T(2,128)(2,1)} %gather_fusion) | copy-start | bytes 6291460
  124.2 38.3 %all-to-all-start.1 = ((bf16[1,128,2,256]{3,2,0,1:T(2,128)(2,1)}), bf16[1,128,2,256]{3,2,0,1:T(2,128)(2,1)S(1)}, u32[]{:S(2)}, u32[]{:S(2)}) async-start(bf16[1,128,2,256]{3,2,0,1:T(2,128)(2,1)} %copy.39), calls=%async_computation.1 | async-start | bytes 262144 | tf_op jit(solution)/shard_map/all_to_all | solution.py:105
Sparse Core Ops, SparseCore 0:
  70.5 24.9 all-gather.1
where the time goes:
time: 171 us
  blocking collectives  57.2 us (33%)
  waiting for transfers between devices  36 us (21%)
  local copies, waits for them, and re-layouts  33.9 us (20%)
  starting transfers between devices  18.6 us (11%)
  between operations  14.3 us (8%)
  other arithmetic  7.53 us (4%)
  matrix products  3.38 us (2%)
    all_to_all x1, blocking collectives, per_device(): lax.all_to_all(spectra, 'band', split_axis=0, concat_axis=2, tiled=True)  57.2 us
    all_gather x1, waiting for transfers between devices, per_device(): lax.all_gather(owned, 'segment', axis=3, tiled=True)  20 us
    all_to_all x1, starting transfers between devices, per_device(): lax.all_to_all(formed_total.astype(jnp.bfloat16), 'band', split_axis=1, c...  18.6 us
    gather x1, local copies, waits for them, and re-layouts, per_device(): jnp.take(lax.all_gather(owned, 'segment', axis=3, tiled=True), slot_of_an...  16.5 us
    all_to_all x1, waiting for transfers between devices, per_device(): lax.all_to_all(formed_total.astype(jnp.bfloat16), 'band', split_axis=1, c...  16.1 us
    all_gather x1, local copies, waits for them, and re-layouts, per_device(): lax.all_gather(owned, 'segment', axis=3, tiled=True)  8.26 us
    another operation x1, other arithmetic  4.98 us
  transfers between devices with their start and end apart: 2, of which 2 were waited for; matrix products, arithmetic and copies ran while one was open for 5% of the time, Pallas kernels for 0%

commit v1 on v0

--- a/solution.py
+++ b/solution.py
@@ -93,7 +93,11 @@
     spectra = paired(channelize(voltages))
     owned = lax.all_to_all(spectra, "band", split_axis=0, concat_axis=2, tiled=True)
     ordered = jnp.take(
-        lax.all_gather(owned, "segment", axis=3, tiled=True), slot_of_antenna, axis=2
+        jnp.concatenate(
+            lax.all_to_all(jnp.stack([owned] * lax.axis_size("segment")), "segment", 0, 0), axis=3
+        ),
+        slot_of_antenna,
+        axis=2,
     )
     gram_part, formed_part = jax.vmap(pair_terms)(ordered, weights, row_starts)
     formed_total = formed_part

time: 171 us -> 148 us (0.87)
  blocking collectives: 57.2 us -> 0 us
  waiting for transfers between devices: 36 us -> 71.5 us
  between operations: 14.3 us -> 0.91 us
  starting transfers between devices: 18.6 us -> 31.2 us
    all_to_all x1 -> x0, blocking collectives: 57.2 us -> none  [per_device(): lax.all_to_all(spectra, 'band', split_axis=0, concat_axis=2, tiled=True)]
    all_to_all x0 -> x2, waiting for transfers between devices: none -> 56.2 us  [the longest x1 35.6 us: per_device(): lax.all_to_all(spectra, 'band', split_axis=0, concat_axis=2, tiled=True)]
    all_to_all x0 -> x2, starting transfers between devices: none -> 25.4 us  [the longest x1 21.6 us: per_device(): lax.all_to_all(spectra, 'band', split_axis=0, concat_axis=2, tiled=True)]
    all_gather x1 -> x0, waiting for transfers between devices: 20 us -> none  [per_device(): lax.all_gather(owned, 'segment', axis=3, tiled=True)]
    all_to_all x1, starting transfers between devices: 18.6 us -> 5.77 us  [per_device(): lax.all_to_all(formed_total.astype(jnp.bfloat16), 'band', split_axis=1, c...]
    all_gather x1 -> x0, local copies, waits for them, and re-layouts: 8.26 us -> none  [per_device(): lax.all_gather(owned, 'segment', axis=3, tiled=True)]
    reshape x0 -> x1, local copies, waits for them, and re-layouts: none -> 4.82 us  [per_device(): jnp.concatenate(lax.all_to_all(jnp.stack([owned] * lax.axis_size('segment...]
    another operation x0 -> x2, local copies, waits for them, and re-layouts: none -> 1.95 us  [per_device(): jnp.stack([owned] * lax.axis_size('segment'))]
  transfers between devices with their start and end apart: 2 -> 3, of which waited for: 2 -> 3; matrix products, arithmetic and copies ran while one was open for 5% -> 6% of each run, Pallas kernels for 0% -> 0%
where the time goes in v1:
time: 148 us
  waiting for transfers between devices  71.5 us (48%)
  local copies, waits for them, and re-layouts  33.3 us (22%)
  starting transfers between devices  31.2 us (21%)
  other arithmetic  7.53 us (5%)
  matrix products  3.38 us (2%)
    all_to_all x1, waiting for transfers between devices, per_device(): lax.all_to_all(spectra, 'band', split_axis=0, concat_axis=2, tiled=True)  35.6 us
    all_to_all x1, starting transfers between devices, per_device(): lax.all_to_all(spectra, 'band', split_axis=0, concat_axis=2, tiled=True)  21.6 us
    all_to_all x1, waiting for transfers between devices, per_device(): lax.all_to_all(jnp.stack([owned] * lax.axis_size('segment')), 'segment',...  20.6 us
    gather x1, local copies, waits for them, and re-layouts, per_device(): jnp.take(jnp.concatenate(lax.all_to_all(jnp.stack([owned] * lax.axis_size...  16.5 us
    all_to_all x1, waiting for transfers between devices, per_device(): lax.all_to_all(formed_total.astype(jnp.bfloat16), 'band', split_axis=1, c...  15.3 us
    all_to_all x1, starting transfers between devices, per_device(): lax.all_to_all(formed_total.astype(jnp.bfloat16), 'band', split_axis=1, c...  5.77 us
    another operation x1, other arithmetic  4.98 us
    reshape x1, local copies, waits for them, and re-layouts, per_device(): jnp.concatenate(lax.all_to_all(jnp.stack([owned] * lax.axis_size('segment...  4.82 us
  transfers between devices with their start and end apart: 3, of which 3 were waited for; matrix products, arithmetic and copies ran while one was open for 6% of the time, Pallas kernels for 0%

profile of v1, /device:TPU:32, one launch (start us, length us, event | category | flops | bytes accessed | tf_op | source)
XLA Modules:
  0.0 147.8 jit_solution(13216757828179900777)
XLA Ops:
  0.6 0.0 copy-start
  0.6 0.1 fusion.41
  0.8 0.2 sine_multiply_fusion
  0.9 1.5 reshape.634
  2.5 0.9 fusion.7
  3.4 0.3 copy.36
  3.7 0.2 broadcast_in_dim.34
  3.9 1.4 reshape.714
  5.3 21.6 %all-to-all-start = ((bf16[128,2,1024]{2,1,0:T(2,128)(2,1)}), bf16[128,2,1024]{2,1,0:T(2,128)(2,1)S(1)}, u32[]{:S(2)}, u32[]{:S(2)}) async-start(bf16[128,2,1024]{2,1,0:T(2,128)(2,1)} %reshape.714), calls=%async_computation | async-start | bytes 1048576 | tf_op jit(solution)/shard_map/all_to_all | solution.py:94
  27.0 35.6 %all-to-all-done = bf16[128,2,1024]{2,1,0:T(2,128)(2,1)S(1)} async-done(((bf16[128,2,1024]{2,1,0:T(2,128)(2,1)}), bf16[128,2,1024]{2,1,0:T(2,128)(2,1)S(1)}, u32[]{:S(2)}, u32[]{:S(2)}) %all-to-all-start) | async-done | bytes 524320 | tf_op jit(solution)/shard_map/all_to_all | solution.py:94
  62.6 0.6 reshape.715
  63.2 0.2 copy.37
  63.4 0.4 copy.38
  63.8 1.6 %stack.77 = bf16[4,1,2,2048,64]{3,4,2,1,0:T(8,128)(2,1)} broadcast(bf16[2,2048,64]{1,2,0:T(8,128)(2,1)S(1)} %copy.38), dimensions={2,3,4} | broadcast | bytes 2621440 | tf_op jit(solution)/shard_map/stack | solution.py:97
  65.4 3.7 %all-to-all-start.1 = ((bf16[4,1,2,2048,64]{3,4,2,1,0:T(8,128)(2,1)}), bf16[4,1,2,2048,64]{3,4,2,1,0:T(8,128)(2,1)S(1)}, u32[]{:S(2)}, u32[]{:S(2)}) async-start(bf16[4,1,2,2048,64]{3,4,2,1,0:T(8,128)(2,1)} %stack.77), calls=%async_computation.1 | async-start | bytes 4194304 | tf_op jit(solution)/shard_map/all_to_all | solution.py:97
  69.1 0.0 copy-done.2
  69.2 5.0 %cosine_convert_fusion = (bf16[1,128,2048]{2,1,0:T(8,128)(2,1)S(1)}, bf16[1,128,2048]{2,1,0:T(8,128)(2,1)S(1)}) fusion(s32[2048]{0:T(1024)S(1)} %bitcast.119, s32[128]{0:T(128)S(1)} %get-tuple-element.51, s32[2048]{0:T(1024)S(1)} %bitcast.118, s32[128]{0:T(128)S(1)} %get-tuple-element.50, s32[]{:T(128)} %bitcast.31), kind=kLoop, calls=%fused_computation.31 | loop fusion | flops 8126464 | bytes 1065988 | tf_op jit(solution)/shard_map/convert
  74.2 20.6 %all-to-all-done.1 = bf16[4,1,2,2048,64]{3,4,2,1,0:T(8,128)(2,1)S(1)} async-done(((bf16[4,1,2,2048,64]{3,4,2,1,0:T(8,128)(2,1)}), bf16[4,1,2,2048,64]{3,4,2,1,0:T(8,128)(2,1)S(1)}, u32[]{:S(2)}, u32[]{:S(2)}) %all-to-all-start.1) | async-done | bytes 2097184 | tf_op jit(solution)/shard_map/all_to_all | solution.py:97
  94.8 1.5 copy.39
  96.3 4.8 %copy.40 = bf16[2,2048,256]{2,0,1:T(2,128)(2,1)S(1)} copy(bf16[2,2048,256]{1,2,0:T(8,128)(2,1)} %bitcast.112) | data formatting | bytes 4194304 | tf_op jit(solution)/shard_map/reshape | solution.py:96
  101.1 16.5 %gather_fusion = bf16[2048,2,256]{2,1,0:T(2,128)(2,1)} fusion(bf16[2,2048,256]{2,0,1:T(2,128)(2,1)S(1)} %copy.40, s32[2048]{0:T(1024)S(1)} %fusion.42), kind=kCustom, calls=%fused_computation | custom fusion | bytes 4202496 | tf_op jit(solution)/shard_map/jit(_take)/gather | solution.py:95
  117.6 2.1 %bitcast_select_fusion = bf16[1,2,2048,256]{3,2,0,1:T(8,128)(2,1)S(1)} fusion(pred[2048]{0:T(1024)(128)(4,1)S(1)} %compare_and_fusion, bf16[2048,2,256]{2,1,0:T(2,128)(2,1)} %gather_fusion), kind=kLoop, calls=%fused_computation.3 | loop fusion | flops 1048576 | bytes 4196352 | tf_op jit(solution)/shard_map/jit(_take)/select_n | solution.py:95
  119.7 0.1 copy-done.1
  119.8 0.9 fusion.8
  120.7 0.8 copy.42
  121.5 5.8 %all-to-all-start.2 = ((bf16[1,128,2,256]{3,2,0,1:T(2,128)(2,1)}), bf16[1,128,2,256]{3,2,0,1:T(2,128)(2,1)S(1)}, u32[]{:S(2)}, u32[]{:S(2)}) async-start(bf16[1,128,2,256]{3,2,0,1:T(2,128)(2,1)} %copy.42), calls=%async_computation.2 | async-start | bytes 262144 | tf_op jit(solution)/shard_map/all_to_all | solution.py:109
  127.4 1.3 fusion
  128.7 2.3 %fusion.47 = (f32[1,1,256,2048]{3,2,1,0:T(8,128)}, f32[1,1,256,2048]{3,2,1,0:T(8,128)}) fusion(f32[1,2,256,2048]{3,2,1,0:T(8,128)S(1)} %fusion), kind=kLoop, calls=%fused_computation.84 | loop fusion | bytes 8388608 | tf_op jit(solution)/shard_map/slice | solution.py:107
  131.0 15.3 %all-to-all-done.2 = bf16[1,128,2,256]{3,2,0,1:T(2,128)(2,1)S(1)} async-done(((bf16[1,128,2,256]{3,2,0,1:T(2,128)(2,1)}), bf16[1,128,2,256]{3,2,0,1:T(2,128)(2,1)S(1)}, u32[]{:S(2)}, u32[]{:S(2)}) %all-to-all-start.2) | async-done | bytes 131104 | tf_op jit(solution)/shard_map/all_to_all | solution.py:109
  146.3 0.3 convolution_bitcast_fusion.1
  146.6 0.2 copy.45
  146.8 1.0 reshape_reshape.3
  (16 shorter events, 0.2 us)
Async XLA Ops:
  0.6 26.3 %copy-start = (s32[1024,2]{0,1:T(2,128)S(1)}, s32[1024,2]{0,1:T(2,128)}, u32[]{:S(2)}) copy-start(s32[1024,2]{0,1:T(2,128)} %param.7) | copy-start | bytes 24580
  5.3 57.3 %all-to-all-start = ((bf16[128,2,1024]{2,1,0:T(2,128)(2,1)}), bf16[128,2,1024]{2,1,0:T(2,128)(2,1)S(1)}, u32[]{:S(2)}, u32[]{:S(2)}) async-start(bf16[128,2,1024]{2,1,0:T(2,128)(2,1)} %reshape.714), calls=%async_computation | async-start | bytes 1048576 | tf_op jit(solution)/shard_map/all_to_all | solution.py:94
  65.4 3.8 %copy-start.2 = (s32[2048]{0:T(1024)S(1)}, s32[2048]{0:T(1024)}, u32[]{:S(2)}) copy-start(s32[2048]{0:T(1024)} %param.5) | copy-start | bytes 24580
  65.4 3.8 %copy-start.3 = (s32[2048,2]{0,1:T(2,128)S(1)}, s32[2048,2]{0,1:T(2,128)}, u32[]{:S(2)}) copy-start(s32[2048,2]{0,1:T(2,128)} %param.6) | copy-start | bytes 49156
  65.4 29.4 %all-to-all-start.1 = ((bf16[4,1,2,2048,64]{3,4,2,1,0:T(8,128)(2,1)}), bf16[4,1,2,2048,64]{3,4,2,1,0:T(8,128)(2,1)S(1)}, u32[]{:S(2)}, u32[]{:S(2)}) async-start(bf16[4,1,2,2048,64]{3,4,2,1,0:T(8,128)(2,1)} %stack.77), calls=%async_computation.1 | async-start | bytes 4194304 | tf_op jit(solution)/shard_map/all_to_all | solution.py:97
  117.6 2.2 %copy-start.1 = (bf16[2048,2,256]{2,1,0:T(2,128)(2,1)S(1)}, bf16[2048,2,256]{2,1,0:T(2,128)(2,1)}, u32[]{:S(2)}) copy-start(bf16[2048,2,256]{2,1,0:T(2,128)(2,1)} %gather_fusion) | copy-start | bytes 6291460
  121.5 24.7 %all-to-all-start.2 = ((bf16[1,128,2,256]{3,2,0,1:T(2,128)(2,1)}), bf16[1,128,2,256]{3,2,0,1:T(2,128)(2,1)S(1)}, u32[]{:S(2)}, u32[]{:S(2)}) async-start(bf16[1,128,2,256]{3,2,0,1:T(2,128)(2,1)} %copy.42), calls=%async_computation.2 | async-start | bytes 262144 | tf_op jit(solution)/shard_map/all_to_all | solution.py:109
